TPU v7x, 256 devices: a whole 4x4x8 slice. The times are simulated.
256 devices in a mesh: group: 32 (over x, y, core), mp: 8 (over z).
Axes of the slice: x: 4, y: 4, z: 8, core: 2. Of those that a mesh axis runs over, the one named last changes fastest.
Arguments:
- hidden: bfloat16 [16384, 1792], P('group')
- norm_gain: float32 [1792], replicated, may hold values from 0.1 to 1.9
- qkv_weight: bfloat16 [1792, 2304], P(None, 'mp'), may hold values from -0.125 to 0.125
- out_weight: bfloat16 [1792, 1792], P('mp'), may hold values from -0.125 to 0.125
- adapter_down: bfloat16 [1792, 1024], P(None, 'mp'), may hold values from -0.125 to 0.125
- adapter_up: bfloat16 [1024, 1792], P('mp'), may hold values from -1.5 to 1.5
- vocab_rows: bfloat16 [4096, 1792], P(('group', 'mp')), may hold values from -0.125 to 0.125
- segments: int32 [16384], P('group'), may hold values from 0 to 127, never falling along the last dimension, each value on 1 to 512 neighbouring positions
- request_adapter: int32 [128], replicated, may hold values from 0 to 63
- adapter_slot: int32 [64], replicated, may hold values from 0 to 63, each once
- page_table: int32 [2048], replicated, may hold values from 0 to 2047, as said below
Outputs:
- layer_update: bfloat16 [16384, 1792], P('group', 'mp')
- state_norms: float32 [16, 16384], P('mp', 'group')
- max_logits: float32 [16384], P(('group', 'mp'))
Inputs may be any that keep to these rules, and one draw needn't show every extreme that they name: A permutation of all pages. Logical page k of group g (entry g * 64 + k) lies in group page_table[g * 64 + k] // 64, and every group holds exactly two of the logical pages of every group. `segments`: every request's tokens stand together and in order; no request has more than 512 tokens. `adapter_slot`: A permutation.
All inputs are finite; a program needn't handle non-finite values.
Results may differ from a plain program's by a relative error of at most 0.013.
Values may be sent and summed in bfloat16 or wider, within the bound.
A program may use at most 64 MiB of HBM per device.

v0:
```python
import jax
import jax.numpy as jnp
from jax import lax
from jax.sharding import PartitionSpec as P

FEAT = 16
HD = 112
RANK = 16
EPSILON = 1e-05
PRECISE = lax.Precision.HIGHEST


def from_behind(value, axis, by):
    size = lax.axis_size(axis)
    pairs = [(i, i + by) for i in range(size) if 0 <= i + by < size]
    return lax.ppermute(value, axis, pairs)


def rms_normed(values, norm_gain):
    wide = values.astype(jnp.float32)
    meansq = jnp.mean(wide * wide, axis=-1, keepdims=True)
    return (wide * lax.rsqrt(meansq + EPSILON) * norm_gain).astype(jnp.bfloat16)


def features(vectors, feat_width):
    linear_part = vectors / feat_width**0.25
    outer_part = (vectors[..., :, None] * vectors[..., None, :]).reshape(
        vectors.shape[:-1] + (feat_width * feat_width,)
    )
    outer_part = outer_part / (2.0 * feat_width) ** 0.5
    ones_part = jnp.ones(vectors.shape[:-1] + (1,), jnp.float32)
    return jnp.concatenate([ones_part, linear_part, outer_part], axis=-1)


def block_step(state_carry, block_inputs, feat_width):
    states, totals, owner_seg = state_carry
    phi_query, phi_key, query_rows, key_rows, value_rows, seg_ids = block_inputs
    scaling = feat_width ** (-0.5)
    block_len = seg_ids.shape[0]
    position = jnp.arange(block_len, dtype=jnp.int32)
    allowed = (
        (position[:, None] >= position[None, :]) & (seg_ids[:, None] == seg_ids[None, :])
    ).astype(jnp.float32)
    carried = (seg_ids == owner_seg).astype(jnp.float32)[None, :]
    scores = jnp.einsum("hcf,hdf->hcd", query_rows, key_rows, precision=PRECISE) * scaling
    weights = (1.0 + scores + 0.5 * scores * scores) * allowed[None]
    numerator = jnp.einsum("hcd,hde->hce", weights, value_rows, precision=PRECISE)
    numerator = numerator + carried[..., None] * jnp.einsum(
        "hcp,hpe->hce", phi_query, states, precision=PRECISE
    )
    denominator = jnp.sum(weights, axis=-1) + carried * jnp.einsum(
        "hcp,hp->hc", phi_query, totals, precision=PRECISE
    )
    mixed_out = numerator / denominator[..., None]
    key_scores = jnp.einsum("hcf,hdf->hcd", key_rows, key_rows, precision=PRECISE) * scaling
    value_gram = jnp.einsum("hce,hde->hcd", value_rows, value_rows, precision=PRECISE)
    key_gram = (1.0 + key_scores + 0.5 * key_scores * key_scores) * value_gram
    masked_gram = jnp.einsum("cd,hde->hce", allowed, key_gram, precision=PRECISE)
    local_squares = jnp.sum(masked_gram * allowed[None], axis=-1)
    along = jnp.sum(
        jnp.einsum("hcp,hpe->hce", phi_key, states, precision=PRECISE) * value_rows, axis=-1
    )
    cross_squares = jnp.einsum("cd,hd->hc", allowed, along, precision=PRECISE)
    state_squares = jnp.sum(states * states, axis=(1, 2))
    squares = carried * (state_squares[:, None] + 2.0 * cross_squares) + local_squares
    counted = carried * totals[:, :1] + jnp.sum(allowed, axis=-1)[None, :]
    state_norm = jnp.sqrt(squares / (counted * (feat_width * value_rows.shape[-1])))
    last_seg = seg_ids[-1]
    member = (seg_ids == last_seg).astype(jnp.float32)
    continues = (owner_seg == last_seg).astype(jnp.float32)
    new_states = continues * states + jnp.einsum(
        "hcp,hce->hpe", phi_key * member[None, :, None], value_rows, precision=PRECISE
    )
    new_totals = continues * totals + jnp.einsum("hcp,c->hp", phi_key, member, precision=PRECISE)
    return ((new_states, new_totals, last_seg), (mixed_out, state_norm))


def best_of(candidates, piece):
    logits = jnp.einsum("rd,vd->rv", candidates, piece, preferred_element_type=jnp.float32)
    return jnp.max(logits, axis=1)


def on_device(
    hidden,
    norm_gain,
    qkv_weight,
    out_weight,
    adapter_down,
    adapter_up,
    vocab_rows,
    segments,
    request_adapter,
    adapter_slot,
    page_table,
):
    groups = lax.axis_size("group")
    own_group = lax.axis_index("group")
    shards = lax.axis_size("mp")
    own_shard = lax.axis_index("mp")
    rows_here = segments.shape[0]
    model_width = hidden.shape[1]
    slice_width = model_width // shards
    table = page_table.reshape(groups, -1)
    per_group = table.shape[1]
    per_peer = per_group // groups
    page_len = rows_here // per_group
    holders = table // per_group
    position = jnp.arange(per_group, dtype=jnp.int32)
    sort_keys = jnp.where(holders == own_group, position[None, :], per_group + position[None, :])
    ranked = jnp.argsort(sort_keys, axis=1)[:, :per_peer]
    picked = jnp.take_along_axis(table, ranked, axis=1) - own_group * per_group
    outgoing = hidden.reshape(per_group, page_len, model_width)[picked]
    normed_pages = rms_normed(outgoing, norm_gain)
    projected_pages = jnp.einsum(
        "abrd,dc->abrc", normed_pages, qkv_weight, preferred_element_type=jnp.float32
    ).astype(jnp.bfloat16)
    lowered_pages = jnp.einsum(
        "abrd,dc->abrc", normed_pages, adapter_down, preferred_element_type=jnp.float32
    ).astype(jnp.bfloat16)
    kept_pages = lax.dynamic_slice_in_dim(outgoing, own_shard * slice_width, slice_width, 3)
    widths = (kept_pages.shape[3], projected_pages.shape[3], lowered_pages.shape[3])
    packed = lax.all_to_all(
        jnp.concatenate([kept_pages, projected_pages, lowered_pages], axis=3),
        "group",
        split_axis=0,
        concat_axis=0,
        tiled=True,
    )
    arrived = (
        packed[..., : widths[0]],
        packed[..., widths[0] : widths[0] + widths[1]],
        packed[..., widths[0] + widths[1] :],
    )
    own_holders = lax.dynamic_index_in_dim(holders, own_group, 0, keepdims=False)
    onehot = (own_holders[:, None] == jnp.arange(groups, dtype=jnp.int32)[None, :]).astype(
        jnp.int32
    )
    earlier = jnp.sum((jnp.cumsum(onehot, axis=0) - onehot) * onehot, axis=1)
    source_rows = own_holders * per_peer + earlier

    def placed(received):
        gathered_rows = received.reshape((groups * per_peer,) + received.shape[2:])[source_rows]
        return gathered_rows.reshape((rows_here,) + received.shape[3:])

    residual, projected, lowered = [placed(received) for received in arrived]
    group_vocab = lax.all_gather(vocab_rows, "group", axis=0, tiled=True)
    heads_here = projected.shape[1] // (2 * FEAT + HD)
    split_heads = jnp.transpose(
        projected.reshape(rows_here, heads_here, 2 * FEAT + HD).astype(jnp.float32), (1, 0, 2)
    )
    query_rows = split_heads[..., :FEAT]
    key_rows = split_heads[..., FEAT : 2 * FEAT]
    value_rows = split_heads[..., 2 * FEAT :]
    phi_query = features(query_rows, FEAT)
    phi_key = features(key_rows, FEAT)
    last_seg = segments[-1]
    member = (segments == last_seg).astype(jnp.float32)
    end_state = jnp.einsum(
        "hcp,hce->hpe", phi_key * member[None, :, None], value_rows, precision=PRECISE
    )
    end_totals = jnp.einsum("hcp,c->hp", phi_key, member, precision=PRECISE)
    end_tag = jnp.reshape(last_seg + 1, (1,)).astype(jnp.float32)
    state_size, totals_size = (end_state.size, end_totals.size)
    handed = from_behind(
        jnp.concatenate([end_state.reshape(-1), end_totals.reshape(-1), end_tag]).astype(
            jnp.bfloat16
        ),
        "group",
        1,
    ).astype(jnp.float32)
    got_state = handed[:state_size].reshape(end_state.shape)
    got_totals = handed[state_size : state_size + totals_size].reshape(end_totals.shape)
    got_tag = handed[state_size + totals_size :]
    initial = (got_state, got_totals, got_tag[0].astype(jnp.int32) - 1)
    block_len = min(256, rows_here)
    blocks = rows_here // block_len

    def regroup(values):
        return jnp.transpose(
            values.reshape(values.shape[0], blocks, block_len, values.shape[-1]), (1, 0, 2, 3)
        )

    scan_inputs = (
        regroup(phi_query),
        regroup(phi_key),
        regroup(query_rows),
        regroup(key_rows),
        regroup(value_rows),
        segments.reshape(blocks, block_len),
    )

    def scan_step(state_carry, block_inputs):
        return block_step(state_carry, block_inputs, FEAT)

    _, (mixed_out, state_norm) = lax.scan(scan_step, initial, scan_inputs)
    attended = (
        jnp.transpose(mixed_out, (0, 2, 1, 3))
        .reshape(rows_here, heads_here * HD)
        .astype(jnp.bfloat16)
    )
    group_vocab, attended = lax.optimization_barrier((group_vocab, attended))
    state_norms = jnp.transpose(state_norm, (1, 0, 2)).reshape(heads_here, rows_here)
    request_ids = jnp.arange(request_adapter.shape[0], dtype=jnp.int32)
    adapter_of = jnp.sum(
        jnp.where(segments[:, None] == request_ids[None, :], request_adapter[None, :], 0), axis=1
    )
    adapter_ids = jnp.arange(adapter_slot.shape[0], dtype=jnp.int32)
    slot_ids = jnp.sum(
        jnp.where(adapter_of[:, None] == adapter_ids[None, :], adapter_slot[None, :], 0), axis=1
    )
    column_slot = jnp.arange(lowered.shape[1], dtype=jnp.int32) // RANK
    local_slot = slot_ids - own_shard * (lowered.shape[1] // RANK)
    low_rank = jnp.where(
        local_slot[:, None] == column_slot[None, :], lowered, jnp.zeros_like(lowered)
    )
    partial_value = jnp.dot(attended, out_weight, preferred_element_type=jnp.float32)
    partial_value = partial_value + jnp.dot(
        low_rank, adapter_up, preferred_element_type=jnp.float32
    )
    summed = lax.psum_scatter(
        partial_value.astype(jnp.bfloat16), "mp", scatter_dimension=1, tiled=True
    )
    final_rows = (residual.astype(jnp.float32) + summed.astype(jnp.float32)).astype(jnp.bfloat16)
    group_rows = lax.all_gather(final_rows, "mp", axis=1, tiled=True)
    partial_best = best_of(group_rows, group_vocab)
    max_logits = lax.dynamic_slice_in_dim(
        lax.pmax(partial_best, "mp"), own_shard * (rows_here // shards), rows_here // shards
    )
    return (summed, state_norms, max_logits)


def solution(mesh):
    placed = (
        P("group", None),
        P(),
        P(None, "mp"),
        P("mp", None),
        P(None, "mp"),
        P("mp", None),
        P(("group", "mp"), None),
        P("group"),
        P(),
        P(),
        P(),
    )
    return jax.shard_map(
        on_device,
        mesh=mesh,
        in_specs=placed,
        out_specs=(P("group", "mp"), P("mp", "group"), P(("group", "mp"))),
        check_vma=False,
    )
```

profile of v0, /device:TPU:2, one launch (start us, length us, event | category | flops | bytes accessed | tf_op | source)
XLA Modules:
  0.0 208.3 jit_solution(18308353681001285271)
XLA Ops:
  11.3 1.9 gather_fusion
  13.2 2.0 fusion.49
  16.6 2.3 %fusion.59 = bf16[32,2,8,128]{3,2,1,0:T(8,128)(2,1)S(1)} fusion(bf16[32,2,8,1792]{3,2,1,0:T(8,128)(2,1)} %bitcast.225, f32[1792]{0:T(1024)S(1)} %copy-done.16, f32[32,2,8]{2,1,0:T(2,128)S(1)} %copy.93, bf16[1792,128]{1,0:T(8,128)(2,1)S(1)} %copy-done.15), kind=kOutput, calls=%fused_computation.84 | convolution fusion | flops 238616576 | bytes 2434048 | tf_op jit(solution)/shard_map/abrd,dc->abrc/dot_general | solution.py:117
  21.3 7.6 %all-to-all-start = ((bf16[32,2,8,640]{3,2,1,0:T(8,128)(2,1)}), bf16[32,2,8,640]{3,2,1,0:T(8,128)(2,1)S(1)}, u32[]{:S(2)}, u32[]{:S(2)}) async-start(bf16[32,2,8,640]{3,2,1,0:T(8,128)(2,1)} %pad_maximum_fusion.2), calls=%async_computation | async-start | bytes 1310720 | tf_op jit(solution)/shard_map/all_to_all | solution.py:122
  31.7 8.4 %all-to-all-done = bf16[32,2,8,640]{3,2,1,0:T(8,128)(2,1)S(1)} async-done(((bf16[32,2,8,640]{3,2,1,0:T(8,128)(2,1)}), bf16[32,2,8,640]{3,2,1,0:T(8,128)(2,1)S(1)}, u32[]{:S(2)}, u32[]{:S(2)}) %all-to-all-start) | async-done | bytes 655392 | tf_op jit(solution)/shard_map/all_to_all | solution.py:122
  40.3 1.4 gather_fusion.1
  41.7 1.2 reshape_reshape.3
  44.1 1.3 gather_fusion.2
  45.7 2.2 %pad_maximum_fusion.1 = (f32[2,512,273]{1,2,0:T(8,128)}, f32[2,512,273]{1,2,0:T(8,128)S(1)}) fusion(f32[2,512,256]{1,2,0:T(8,128)S(1)} %bitcast.227, f32[2,512,16]{1,2,0:T(8,128)} %get-tuple-element.273, f32[273]{0:T(512)S(1)} %pad.3.clone, f32[2,512,256]{1,2,0:T(8,128)S(1)} %bitcast.228, f32[2,512,16]{1,2,0:T(8,128)} %get-tuple-element.274), kind=kLoop, calls=%fused_computation.86 | loop fusion | flops 1118208 | bytes 4465732 | tf_op jit(solution)/shard_map/concatenate | solution.py:32
  47.9 1.7 reshape.256
  49.6 2.3 %convolution_convert_fusion = bf16[2,273,112]{2,1,0:T(8,128)(2,1)} fusion(f32[2,512,273]{1,2,0:T(8,128)S(1)} %get-tuple-element.280, f32[512]{0:T(512)S(1)} %get-tuple-element.265, bf16[2,512,144]{1,2,0:T(8,128)(2,1)} %bitcast.230), kind=kOutput, calls=%fused_computation.83 | convolution fusion | flops 376058592 | bytes 1471936 | tf_op jit(solution)/shard_map/hcp,hce->hpe/dot_general | solution.py:158
  51.9 1.8 reshape.251
  53.7 3.0 %reshape.260 = f32[2,2,256,273]{2,1,3,0:T(2,128)} reshape(f32[2,512,273]{1,2,0:T(8,128)} %get-tuple-element.279) | data formatting | bytes 2236416 | tf_op jit(solution)/shard_map/reshape | solution.py:180
  57.4 2.1 concatenate.15
  59.5 2.9 %collective-permute-start = (bf16[61699]{0:T(1024)(128)(2,1)S(1)}, bf16[61699]{0:T(1024)(128)(2,1)S(1)}, u32[]{:S(2)}, u32[]{:S(2)}) collective-permute-start(bf16[61699]{0:T(1024)(128)(2,1)S(1)} %concatenate.15), channel_id=1, source_target_pairs={{0,8},{8,16},{16,24},{24,32},{32,40},{40,48},{48,56},{56,64},{64,7... | collective-permute-start | bytes 370202 | tf_op jit(solution)/shard_map/ppermute | solution.py:16
  63.3 4.5 %collective-permute-done = bf16[61699]{0:T(1024)(128)(2,1)S(1)} collective-permute-done((bf16[61699]{0:T(1024)(128)(2,1)S(1)}, bf16[61699]{0:T(1024)(128)(2,1)S(1)}, u32[]{:S(2)}, u32[]{:S(2)}) %collective-permute-start) | collective-permute-done | bytes 123430 | tf_op jit(solution)/shard_map/ppermute | solution.py:16
  69.6 24.2 %while.21 = (s32[]{:T(128)}, f32[2,273,112]{2,1,0:T(8,128)S(1)}, f32[2,273]{0,1:T(8,128)S(1)}, s32[]{:T(128)}, bf16[2,2,256,112]{2,3,1,0:T(8,128)(2,1)}, /*index...) while((s32[]{:T(128)}, f32[2,273,112]{2,1,0:T(8,128)S(1)}, ...), condition=%wide.region_10.11_spmd, body=%wide.region_4.10_spmd.sunk | while | flops 1377437056 | bytes 23302216 | solution.py:195
  95.1 1.9 fusion.81
  97.1 2.0 add_convert_fusion
  100.8 40.0 %reduce-scatter.2.cloned.1.call-done = bf16[512,224]{0,1:T(8,128)(2,1)} async-done(((bf16[512,1792]{0,1:T(8,128)(2,1)}), bf16[512,224]{0,1:T(8,128)(2,1)}) %reduce-scatter.2.cloned.1.call-update) | async-done | bytes 229392 | tf_op jit(solution)/shard_map/reduce_scatter | solution.py:220
  140.9 1.7 add_convert_fusion.1
  142.6 39.3 %all-gather.5.cloned.1.call-done = bf16[512,1792]{0,1:T(8,128)(2,1)} async-done(((bf16[512,224]{0,1:T(8,128)(2,1)}), bf16[512,1792]{0,1:T(8,128)(2,1)}) %all-gather.5.cloned.1.call-update) | async-done | bytes 1835024 | tf_op jit(solution)/shard_map/all_gather | solution.py:224
  181.9 3.2 %convolution_reduce_fusion = f32[512]{0:T(512)S(1)} fusion(bf16[512,1792]{1,0:T(8,128)(2,1)} %all-gather.3.cloned.1.call-done, bf16[512,1792]{0,1:T(8,128)(2,1)} %all-gather.5.cloned.1.call-done), kind=kOutput, calls=%fused_computation.82 | convolution fusion | flops 939785728 | bytes 3672064 | tf_op jit(solution)/shard_map/rd,vd->rv/dot_general | solution.py:79
  185.1 16.1 %pmax.7 = f32[512]{0:T(512)S(1)} all-reduce(f32[512]{0:T(512)S(1)} %convolution_reduce_fusion), channel_id=1, replica_groups=mesh['group'=32,'mp'=8] {'mp'}, use_global_device_ids=true, to_apply=%region_15.16 | all-reduce | flops 512 | bytes 4096 | tf_op jit(solution)/shard_map/pmax | solution.py:227
  (164 shorter events, 39.0 us)
Async XLA Ops:
  7.2 4.1 %copy-start = (bf16[512,1792]{1,0:T(8,128)(2,1)S(1)}, bf16[512,1792]{1,0:T(8,128)(2,1)}, u32[]{:S(2)}) copy-start(bf16[512,1792]{1,0:T(8,128)(2,1)} %param.13) | copy-start | bytes 5505028
  7.2 87.9 %all-gather.3.cloned.1.call-start = ((), (), s32[]{:S(2)}) async-start(), calls=%async_computation.2 | async-start | bytes 1892352 | tf_op jit(solution)/shard_map/all_gather | solution.py:146
  13.2 3.3 %copy-start.15 = (bf16[1792,128]{1,0:T(8,128)(2,1)S(1)}, bf16[1792,128]{1,0:T(8,128)(2,1)}, u32[]{:S(2)}) copy-start(bf16[1792,128]{1,0:T(8,128)(2,1)} %param.17) | copy-start | bytes 1376260
  13.2 3.3 %copy-start.16 = (f32[1792]{0:T(1024)S(1)}, f32[1792]{0:T(1024)}, u32[]{:S(2)}) copy-start(f32[1792]{0:T(1024)} %param.14) | copy-start | bytes 21508
  16.5 2.4 %copy-start.3 = (bf16[64,8,1792]{2,1,0:T(8,128)(2,1)S(1)}, bf16[64,8,1792]{2,1,0:T(8,128)(2,1)}, u32[]{:S(2)}) copy-start(bf16[64,8,1792]{2,1,0:T(8,128)(2,1)} %gather_fusion) | copy-start | bytes 5505028
  16.6 2.4 %copy-start.14 = (bf16[1792,288]{0,1:T(8,128)(2,1)S(1)}, bf16[1792,288]{0,1:T(8,128)(2,1)}, u32[]{:S(2)}) copy-start(bf16[1792,288]{0,1:T(8,128)(2,1)} %param.15) | copy-start | bytes 3096580
  20.1 8.9 %copy-start.11 = (s32[512]{0:T(512)S(1)}, s32[512]{0:T(512)}, u32[]{:S(2)}) copy-start(s32[512]{0:T(512)} %param.20) | copy-start | bytes 6148
  20.1 11.2 %copy-start.12 = (s32[128]{0:T(128)S(1)}, s32[128]{0:T(128)}, u32[]{:S(2)}) copy-start(s32[128]{0:T(128)} %param.21) | copy-start | bytes 1540
  20.1 11.4 %copy-start.13 = (s32[64]{0:T(128)S(1)}, s32[64]{0:T(128)}, u32[]{:S(2)}) copy-start(s32[64]{0:T(128)} %param.22) | copy-start | bytes 772
  21.3 18.8 %all-to-all-start = ((bf16[32,2,8,640]{3,2,1,0:T(8,128)(2,1)}), bf16[32,2,8,640]{3,2,1,0:T(8,128)(2,1)S(1)}, u32[]{:S(2)}, u32[]{:S(2)}) async-start(bf16[32,2,8,640]{3,2,1,0:T(8,128)(2,1)} %pad_maximum_fusion.2), calls=%async_computation | async-start | bytes 1310720 | tf_op jit(solution)/shard_map/all_to_all | solution.py:122
  28.9 112.0 %reduce-scatter.2.cloned.1.call-start = ((), (), s32[]{:S(2)}) async-start(), calls=%async_computation.3 | async-start | bytes 2064384 | tf_op jit(solution)/shard_map/reduce_scatter | solution.py:220
  40.1 4.0 %copy-start.4 = (bf16[32,2,8,640]{3,2,1,0:T(8,128)(2,1)}, bf16[32,2,8,640]{3,2,1,0:T(8,128)(2,1)S(1)}, u32[]{:S(2)}) copy-start(bf16[32,2,8,640]{3,2,1,0:T(8,128)(2,1)S(1)} %all-to-all-done) | copy-start | bytes 1966084
  43.3 2.4 %copy-start.5 = (bf16[512,2,144]{0,2,1:T(8,128)(2,1)}, bf16[512,2,144]{0,2,1:T(8,128)(2,1)S(1)}, u32[]{:S(2)}) copy-start(bf16[512,2,144]{0,2,1:T(8,128)(2,1)S(1)} %copy.94) | copy-start | bytes 884740
  59.5 8.3 %collective-permute-start = (bf16[61699]{0:T(1024)(128)(2,1)S(1)}, bf16[61699]{0:T(1024)(128)(2,1)S(1)}, u32[]{:S(2)}, u32[]{:S(2)}) collective-permute-start(bf16[61699]{0:T(1024)(128)(2,1)S(1)} %concatenate.15), channel_id=1, source_target_pairs={{0,8},{8,16},{16,24},{24,32},{32,40},{40,48},{48,56},{56,64},{64,7... | collective-permute-start | bytes 370202 | tf_op jit(solution)/shard_map/ppermute | solution.py:16
  72.3 2.6 %copy-start.1 = (f32[2,2,256,273]{2,0,3,1:T(2,128)S(1)}, f32[2,2,256,273]{2,0,3,1:T(2,128)}, u32[]{:S(2)}) copy-start(f32[2,2,256,273]{2,0,3,1:T(2,128)} %get-tuple-element.411) | copy-start | bytes 3354628 | tf_op jit(solution)/shard_map/while
  72.3 2.6 %copy-start.2 = (f32[2,2,256,273]{2,0,3,1:T(2,128)S(1)}, f32[2,2,256,273]{2,0,3,1:T(2,128)}, u32[]{:S(2)}) copy-start(f32[2,2,256,273]{2,0,3,1:T(2,128)} %get-tuple-element.415) | copy-start | bytes 3354628 | tf_op jit(solution)/shard_map/while
  74.8 2.5 %copy-start.9 = (bf16[2,2,256,112]{2,3,1,0:T(8,128)(2,1)S(1)}, bf16[2,2,256,112]{2,3,1,0:T(8,128)(2,1)}, u32[]{:S(2)}) copy-start(bf16[2,2,256,112]{2,3,1,0:T(8,128)(2,1)} %get-tuple-element.393) | copy-start | bytes 688132 | tf_op jit(solution)/shard_map/while
  77.8 3.3 %copy-start.10 = (bf16[2,2,256,112]{2,3,1,0:T(8,128)(2,1)}, bf16[2,2,256,112]{2,3,1,0:T(8,128)(2,1)S(1)}, u32[]{:S(2)}) copy-start(bf16[2,2,256,112]{2,3,1,0:T(8,128)(2,1)S(1)} %fusion.139) | copy-start | bytes 688132 | tf_op jit(solution)/shard_map/while
  84.4 2.6 %copy-start.1 = (f32[2,2,256,273]{2,0,3,1:T(2,128)S(1)}, f32[2,2,256,273]{2,0,3,1:T(2,128)}, u32[]{:S(2)}) copy-start(f32[2,2,256,273]{2,0,3,1:T(2,128)} %get-tuple-element.411) | copy-start | bytes 3354628 | tf_op jit(solution)/shard_map/while
  84.4 2.6 %copy-start.2 = (f32[2,2,256,273]{2,0,3,1:T(2,128)S(1)}, f32[2,2,256,273]{2,0,3,1:T(2,128)}, u32[]{:S(2)}) copy-start(f32[2,2,256,273]{2,0,3,1:T(2,128)} %get-tuple-element.415) | copy-start | bytes 3354628 | tf_op jit(solution)/shard_map/while
  86.9 2.5 %copy-start.9 = (bf16[2,2,256,112]{2,3,1,0:T(8,128)(2,1)S(1)}, bf16[2,2,256,112]{2,3,1,0:T(8,128)(2,1)}, u32[]{:S(2)}) copy-start(bf16[2,2,256,112]{2,3,1,0:T(8,128)(2,1)} %get-tuple-element.393) | copy-start | bytes 688132 | tf_op jit(solution)/shard_map/while
  89.9 3.3 %copy-start.10 = (bf16[2,2,256,112]{2,3,1,0:T(8,128)(2,1)}, bf16[2,2,256,112]{2,3,1,0:T(8,128)(2,1)S(1)}, u32[]{:S(2)}) copy-start(bf16[2,2,256,112]{2,3,1,0:T(8,128)(2,1)S(1)} %fusion.139) | copy-start | bytes 688132 | tf_op jit(solution)/shard_map/while
  93.8 3.2 %copy-start.17 = (f32[2,2,256]{2,1,0:T(2,128)}, f32[2,2,256]{2,1,0:T(2,128)S(1)}, u32[]{:S(2)}) copy-start(f32[2,2,256]{2,1,0:T(2,128)S(1)} %get-tuple-element.189) | copy-start | bytes 12292
  99.1 82.8 %all-gather.5.cloned.1.call-start = ((), (), s32[]{:S(2)}) async-start(), calls=%async_computation.4 | async-start | bytes 2064384 | tf_op jit(solution)/shard_map/all_gather | solution.py:224
  (4 other events, 6.5 us)
Sparse Core Ops, SparseCore 0:
  10.6 54.6 all-gather.2
  99.2 41.6 reduce-scatter.1
  142.7 39.1 all-gather.4
where the time goes:
time: 209 us; the launch traced here: 208 us
  waiting for transfers between devices  93 us (44%)
  local copies, waits for them, and re-layouts  29 us (14%)
  matrix products  28.1 us (13%)
  blocking collectives  16.1 us (8%)
  between operations  15.6 us (7%)
  other arithmetic  12.8 us (6%)
  starting transfers between devices  10.7 us (5%)
  loops' own time  2.99 us (1%)
    reduce_scatter x1, waiting for transfers between devices, on_device(): lax.psum_scatter(partial_value.astype(jnp.bfloat16), 'mp', scatter_dimens...  40 us
    all_gather x1, waiting for transfers between devices, on_device(): group_rows = lax.all_gather(final_rows, 'mp', axis=1, tiled=True)  39.3 us
    pmax x1, blocking collectives, on_device(): lax.pmax(partial_best, 'mp')  16.1 us
    all_to_all x1, waiting for transfers between devices, on_device(): lax.all_to_all(jnp.concatenate([kept_pages, projected_pages, lowered_page...  8.43 us
    all_to_all x1, starting transfers between devices, on_device(): lax.all_to_all(jnp.concatenate([kept_pages, projected_pages, lowered_page...  7.62 us
    reshape x3, local copies, waits for them, and re-layouts, regroup(): values.reshape(values.shape[0], blocks, block_len, values.shape[-1])  4.69 us
    ppermute x1, waiting for transfers between devices, from_behind(): return lax.ppermute(value, axis, pairs)  4.52 us
  transfers between devices with their start and end apart: 5, of which 4 were waited for; matrix products, arithmetic and copies ran while one was open for 29% of the time, Pallas kernels for 0%

commit v1 on v0

--- a/solution.py
+++ b/solution.py
@@ -221,7 +221,9 @@
         partial_value.astype(jnp.bfloat16), "mp", scatter_dimension=1, tiled=True
     )
     final_rows = (residual.astype(jnp.float32) + summed.astype(jnp.float32)).astype(jnp.bfloat16)
-    group_rows = lax.all_gather(final_rows, "mp", axis=1, tiled=True)
+    group_rows = jnp.concatenate(
+        lax.all_to_all(jnp.stack([final_rows] * lax.axis_size("mp")), "mp", 0, 0), axis=1
+    )
     partial_best = best_of(group_rows, group_vocab)
     max_logits = lax.dynamic_slice_in_dim(
         lax.pmax(partial_best, "mp"), own_shard * (rows_here // shards), rows_here // shards

time: 209 us -> 216 us (1.033)
  starting transfers between devices: 10.7 us -> 15 us
  waiting for transfers between devices: 93 us -> 96 us
    all_to_all x0 -> x1, waiting for transfers between devices: none -> 42.3 us  [on_device(): lax.all_to_all(jnp.stack([final_rows] * lax.axis_size('mp')), 'mp', 0, 0)]
    all_gather x1 -> x0, waiting for transfers between devices: 39.3 us -> none  [on_device(): group_rows = lax.all_gather(final_rows, 'mp', axis=1, tiled=True)]
    all_to_all x0 -> x1, starting transfers between devices: none -> 4.33 us  [on_device(): lax.all_to_all(jnp.stack([final_rows] * lax.axis_size('mp')), 'mp', 0, 0)]
  transfers between devices with their start and end apart: 5 -> 5, of which waited for: 4 -> 4; matrix products, arithmetic and copies ran while one was open for 29% -> 28% of each run, Pallas kernels for 0% -> 0%
where the time goes in v1:
time: 216 us; the launch traced here: 215 us
  waiting for transfers between devices  96 us (44%)
  local copies, waits for them, and re-layouts  30.4 us (14%)
  matrix products  28.1 us (13%)
  between operations  15.9 us (7%)
  starting transfers between devices  15 us (7%)
  blocking collectives  14.7 us (7%)
  other arithmetic  12.1 us (6%)
  loops' own time  2.99 us (1%)
    all_to_all x1, waiting for transfers between devices, on_device(): lax.all_to_all(jnp.stack([final_rows] * lax.axis_size('mp')), 'mp', 0, 0)  42.3 us
    reduce_scatter x1, waiting for transfers between devices, on_device(): lax.psum_scatter(partial_value.astype(jnp.bfloat16), 'mp', scatter_dimens...  40 us
    pmax x1, blocking collectives, on_device(): lax.pmax(partial_best, 'mp')  14.7 us
    all_to_all x1, waiting for transfers between devices, on_device(): lax.all_to_all(jnp.concatenate([kept_pages, projected_pages, lowered_page...  8.43 us
    all_to_all x1, starting transfers between devices, on_device(): lax.all_to_all(jnp.concatenate([kept_pages, projected_pages, lowered_page...  7.62 us
    reshape x3, local copies, waits for them, and re-layouts, regroup(): values.reshape(values.shape[0], blocks, block_len, values.shape[-1])  4.69 us
    ppermute x1, waiting for transfers between devices, from_behind(): return lax.ppermute(value, axis, pairs)  4.52 us
    all_to_all x1, starting transfers between devices, on_device(): lax.all_to_all(jnp.stack([final_rows] * lax.axis_size('mp')), 'mp', 0, 0)  4.33 us
  transfers between devices with their start and end apart: 5, of which 4 were waited for; matrix products, arithmetic and copies ran while one was open for 28% of the time, Pallas kernels for 0%

profile of v1, /device:TPU:2, one launch (start us, length us, event | category | flops | bytes accessed | tf_op | source)
XLA Modules:
  0.0 215.3 jit_solution(14951046541035961520)
XLA Ops:
  11.3 1.9 gather_fusion
  13.2 2.0 fusion.49
  16.6 2.3 %fusion.59 = bf16[32,2,8,128]{3,2,1,0:T(8,128)(2,1)S(1)} fusion(bf16[32,2,8,1792]{3,2,1,0:T(8,128)(2,1)} %bitcast.228, f32[1792]{0:T(1024)S(1)} %copy-done.16, f32[32,2,8]{2,1,0:T(2,128)S(1)} %copy.94, bf16[1792,128]{1,0:T(8,128)(2,1)S(1)} %copy-done.15), kind=kOutput, calls=%fused_computation.84 | convolution fusion | flops 238616576 | bytes 2434048 | tf_op jit(solution)/shard_map/abrd,dc->abrc/dot_general | solution.py:117
  21.3 7.6 %all-to-all-start = ((bf16[32,2,8,640]{3,2,1,0:T(8,128)(2,1)}), bf16[32,2,8,640]{3,2,1,0:T(8,128)(2,1)S(1)}, u32[]{:S(2)}, u32[]{:S(2)}) async-start(bf16[32,2,8,640]{3,2,1,0:T(8,128)(2,1)} %pad_maximum_fusion.2), calls=%async_computation | async-start | bytes 1310720 | tf_op jit(solution)/shard_map/all_to_all | solution.py:122
  31.7 8.4 %all-to-all-done = bf16[32,2,8,640]{3,2,1,0:T(8,128)(2,1)S(1)} async-done(((bf16[32,2,8,640]{3,2,1,0:T(8,128)(2,1)}), bf16[32,2,8,640]{3,2,1,0:T(8,128)(2,1)S(1)}, u32[]{:S(2)}, u32[]{:S(2)}) %all-to-all-start) | async-done | bytes 655392 | tf_op jit(solution)/shard_map/all_to_all | solution.py:122
  40.3 1.4 gather_fusion.1
  44.1 1.3 gather_fusion.2
  45.7 2.2 %pad_maximum_fusion.1 = (f32[2,512,273]{1,2,0:T(8,128)}, f32[2,512,273]{1,2,0:T(8,128)S(1)}) fusion(f32[2,512,256]{1,2,0:T(8,128)S(1)} %bitcast.230, f32[2,512,16]{1,2,0:T(8,128)} %get-tuple-element.273, f32[273]{0:T(512)S(1)} %pad.3.clone, f32[2,512,256]{1,2,0:T(8,128)S(1)} %bitcast.231, f32[2,512,16]{1,2,0:T(8,128)} %get-tuple-element.274), kind=kLoop, calls=%fused_computation.86 | loop fusion | flops 1118208 | bytes 4465732 | tf_op jit(solution)/shard_map/concatenate | solution.py:32
  47.9 1.7 reshape.264
  49.6 2.3 %convolution_convert_fusion = bf16[2,273,112]{2,1,0:T(8,128)(2,1)} fusion(f32[2,512,273]{1,2,0:T(8,128)S(1)} %get-tuple-element.280, f32[512]{0:T(512)S(1)} %get-tuple-element.265, bf16[2,512,144]{1,2,0:T(8,128)(2,1)} %bitcast.233), kind=kOutput, calls=%fused_computation.83 | convolution fusion | flops 376058592 | bytes 1471936 | tf_op jit(solution)/shard_map/hcp,hce->hpe/dot_general | solution.py:158
  51.9 1.8 reshape.259
  53.7 3.0 %reshape.268 = f32[2,2,256,273]{2,1,3,0:T(2,128)} reshape(f32[2,512,273]{1,2,0:T(8,128)} %get-tuple-element.279) | data formatting | bytes 2236416 | tf_op jit(solution)/shard_map/reshape | solution.py:180
  57.4 2.1 concatenate.15
  59.5 2.9 %collective-permute-start = (bf16[61699]{0:T(1024)(128)(2,1)S(1)}, bf16[61699]{0:T(1024)(128)(2,1)S(1)}, u32[]{:S(2)}, u32[]{:S(2)}) collective-permute-start(bf16[61699]{0:T(1024)(128)(2,1)S(1)} %concatenate.15), channel_id=1, source_target_pairs={{0,8},{8,16},{16,24},{24,32},{32,40},{40,48},{48,56},{56,64},{64,7... | collective-permute-start | bytes 370202 | tf_op jit(solution)/shard_map/ppermute | solution.py:16
  63.3 4.5 %collective-permute-done = bf16[61699]{0:T(1024)(128)(2,1)S(1)} collective-permute-done((bf16[61699]{0:T(1024)(128)(2,1)S(1)}, bf16[61699]{0:T(1024)(128)(2,1)S(1)}, u32[]{:S(2)}, u32[]{:S(2)}) %collective-permute-start) | collective-permute-done | bytes 123430 | tf_op jit(solution)/shard_map/ppermute | solution.py:16
  69.6 24.2 %while.21 = (s32[]{:T(128)}, f32[2,273,112]{2,1,0:T(8,128)S(1)}, f32[2,273]{0,1:T(8,128)S(1)}, s32[]{:T(128)}, bf16[2,2,256,112]{2,3,1,0:T(8,128)(2,1)}, /*index...) while((s32[]{:T(128)}, f32[2,273,112]{2,1,0:T(8,128)S(1)}, ...), condition=%wide.region_10.11_spmd, body=%wide.region_4.10_spmd.sunk | while | flops 1377437056 | bytes 23302216 | solution.py:195
  95.1 1.9 fusion.81
  97.1 2.0 add_convert_fusion
  100.8 40.0 %reduce-scatter.2.cloned.1.call-done = bf16[512,224]{0,1:T(8,128)(2,1)} async-done(((bf16[512,1792]{0,1:T(8,128)(2,1)}), bf16[512,224]{0,1:T(8,128)(2,1)}) %reduce-scatter.2.cloned.1.call-update) | async-done | bytes 229392 | tf_op jit(solution)/shard_map/reduce_scatter | solution.py:220
  141.9 1.4 stack.2
  143.3 4.3 %all-to-all-start.1 = ((bf16[8,512,224]{1,2,0:T(8,128)(2,1)}), bf16[8,512,224]{1,2,0:T(8,128)(2,1)}, u32[]{:S(2)}, u32[]{:S(2)}) async-start(bf16[8,512,224]{1,2,0:T(8,128)(2,1)} %stack.2), calls=%async_computation.2 | async-start | bytes 3670016 | tf_op jit(solution)/shard_map/all_to_all | solution.py:225
  147.6 42.3 %all-to-all-done.1 = bf16[8,512,224]{1,2,0:T(8,128)(2,1)} async-done(((bf16[8,512,224]{1,2,0:T(8,128)(2,1)}), bf16[8,512,224]{1,2,0:T(8,128)(2,1)}, u32[]{:S(2)}, u32[]{:S(2)}) %all-to-all-start.1) | async-done | bytes 1835040 | tf_op jit(solution)/shard_map/all_to_all | solution.py:225
  190.0 3.2 %convolution_reduce_fusion = f32[512]{0:T(512)S(1)} fusion(bf16[512,1792]{1,0:T(8,128)(2,1)} %all-gather.2.cloned.1.call-done, bf16[512,1792]{0,1:T(8,128)(2,1)} %bitcast.48), kind=kOutput, calls=%fused_computation.82 | convolution fusion | flops 939785728 | bytes 3672064 | tf_op jit(solution)/shard_map/rd,vd->rv/dot_general | solution.py:79
  193.1 14.7 %pmax.7 = f32[512]{0:T(512)S(1)} all-reduce(f32[512]{0:T(512)S(1)} %convolution_reduce_fusion), channel_id=1, replica_groups=mesh['group'=32,'mp'=8] {'mp'}, use_global_device_ids=true, to_apply=%region_15.16 | all-reduce | flops 512 | bytes 4096 | tf_op jit(solution)/shard_map/pmax | solution.py:229
  (164 shorter events, 41.2 us)
Async XLA Ops:
  7.2 4.1 %copy-start = (bf16[512,1792]{1,0:T(8,128)(2,1)S(1)}, bf16[512,1792]{1,0:T(8,128)(2,1)}, u32[]{:S(2)}) copy-start(bf16[512,1792]{1,0:T(8,128)(2,1)} %param.13) | copy-start | bytes 5505028
  7.2 87.9 %all-gather.2.cloned.1.call-start = ((), (), s32[]{:S(2)}) async-start(), calls=%async_computation.3 | async-start | bytes 1892352 | tf_op jit(solution)/shard_map/all_gather | solution.py:146
  13.2 3.3 %copy-start.15 = (bf16[1792,128]{1,0:T(8,128)(2,1)S(1)}, bf16[1792,128]{1,0:T(8,128)(2,1)}, u32[]{:S(2)}) copy-start(bf16[1792,128]{1,0:T(8,128)(2,1)} %param.17) | copy-start | bytes 1376260
  13.2 3.3 %copy-start.16 = (f32[1792]{0:T(1024)S(1)}, f32[1792]{0:T(1024)}, u32[]{:S(2)}) copy-start(f32[1792]{0:T(1024)} %param.14) | copy-start | bytes 21508
  16.5 2.4 %copy-start.3 = (bf16[64,8,1792]{2,1,0:T(8,128)(2,1)S(1)}, bf16[64,8,1792]{2,1,0:T(8,128)(2,1)}, u32[]{:S(2)}) copy-start(bf16[64,8,1792]{2,1,0:T(8,128)(2,1)} %gather_fusion) | copy-start | bytes 5505028
  16.6 2.4 %copy-start.14 = (bf16[1792,288]{0,1:T(8,128)(2,1)S(1)}, bf16[1792,288]{0,1:T(8,128)(2,1)}, u32[]{:S(2)}) copy-start(bf16[1792,288]{0,1:T(8,128)(2,1)} %param.15) | copy-start | bytes 3096580
  20.1 8.9 %copy-start.11 = (s32[512]{0:T(512)S(1)}, s32[512]{0:T(512)}, u32[]{:S(2)}) copy-start(s32[512]{0:T(512)} %param.20) | copy-start | bytes 6148
  20.1 11.2 %copy-start.12 = (s32[128]{0:T(128)S(1)}, s32[128]{0:T(128)}, u32[]{:S(2)}) copy-start(s32[128]{0:T(128)} %param.21) | copy-start | bytes 1540
  20.1 11.4 %copy-start.13 = (s32[64]{0:T(128)S(1)}, s32[64]{0:T(128)}, u32[]{:S(2)}) copy-start(s32[64]{0:T(128)} %param.22) | copy-start | bytes 772
  21.3 18.8 %all-to-all-start = ((bf16[32,2,8,640]{3,2,1,0:T(8,128)(2,1)}), bf16[32,2,8,640]{3,2,1,0:T(8,128)(2,1)S(1)}, u32[]{:S(2)}, u32[]{:S(2)}) async-start(bf16[32,2,8,640]{3,2,1,0:T(8,128)(2,1)} %pad_maximum_fusion.2), calls=%async_computation | async-start | bytes 1310720 | tf_op jit(solution)/shard_map/all_to_all | solution.py:122
  28.9 112.0 %reduce-scatter.2.cloned.1.call-start = ((), (), s32[]{:S(2)}) async-start(), calls=%async_computation.4 | async-start | bytes 2064384 | tf_op jit(solution)/shard_map/reduce_scatter | solution.py:220
  40.1 4.0 %copy-start.4 = (bf16[32,2,8,640]{3,2,1,0:T(8,128)(2,1)}, bf16[32,2,8,640]{3,2,1,0:T(8,128)(2,1)S(1)}, u32[]{:S(2)}) copy-start(bf16[32,2,8,640]{3,2,1,0:T(8,128)(2,1)S(1)} %all-to-all-done) | copy-start | bytes 1966084
  43.3 2.4 %copy-start.5 = (bf16[512,2,144]{0,2,1:T(8,128)(2,1)}, bf16[512,2,144]{0,2,1:T(8,128)(2,1)S(1)}, u32[]{:S(2)}) copy-start(bf16[512,2,144]{0,2,1:T(8,128)(2,1)S(1)} %copy.95) | copy-start | bytes 884740
  59.5 8.3 %collective-permute-start = (bf16[61699]{0:T(1024)(128)(2,1)S(1)}, bf16[61699]{0:T(1024)(128)(2,1)S(1)}, u32[]{:S(2)}, u32[]{:S(2)}) collective-permute-start(bf16[61699]{0:T(1024)(128)(2,1)S(1)} %concatenate.15), channel_id=1, source_target_pairs={{0,8},{8,16},{16,24},{24,32},{32,40},{40,48},{48,56},{56,64},{64,7... | collective-permute-start | bytes 370202 | tf_op jit(solution)/shard_map/ppermute | solution.py:16
  72.3 2.6 %copy-start.1 = (f32[2,2,256,273]{2,0,3,1:T(2,128)S(1)}, f32[2,2,256,273]{2,0,3,1:T(2,128)}, u32[]{:S(2)}) copy-start(f32[2,2,256,273]{2,0,3,1:T(2,128)} %get-tuple-element.411) | copy-start | bytes 3354628 | tf_op jit(solution)/shard_map/while
  72.3 2.6 %copy-start.2 = (f32[2,2,256,273]{2,0,3,1:T(2,128)S(1)}, f32[2,2,256,273]{2,0,3,1:T(2,128)}, u32[]{:S(2)}) copy-start(f32[2,2,256,273]{2,0,3,1:T(2,128)} %get-tuple-element.415) | copy-start | bytes 3354628 | tf_op jit(solution)/shard_map/while
  74.8 2.5 %copy-start.9 = (bf16[2,2,256,112]{2,3,1,0:T(8,128)(2,1)S(1)}, bf16[2,2,256,112]{2,3,1,0:T(8,128)(2,1)}, u32[]{:S(2)}) copy-start(bf16[2,2,256,112]{2,3,1,0:T(8,128)(2,1)} %get-tuple-element.393) | copy-start | bytes 688132 | tf_op jit(solution)/shard_map/while
  77.8 3.3 %copy-start.10 = (bf16[2,2,256,112]{2,3,1,0:T(8,128)(2,1)}, bf16[2,2,256,112]{2,3,1,0:T(8,128)(2,1)S(1)}, u32[]{:S(2)}) copy-start(bf16[2,2,256,112]{2,3,1,0:T(8,128)(2,1)S(1)} %fusion.139) | copy-start | bytes 688132 | tf_op jit(solution)/shard_map/while
  84.4 2.6 %copy-start.1 = (f32[2,2,256,273]{2,0,3,1:T(2,128)S(1)}, f32[2,2,256,273]{2,0,3,1:T(2,128)}, u32[]{:S(2)}) copy-start(f32[2,2,256,273]{2,0,3,1:T(2,128)} %get-tuple-element.411) | copy-start | bytes 3354628 | tf_op jit(solution)/shard_map/while
  84.4 2.6 %copy-start.2 = (f32[2,2,256,273]{2,0,3,1:T(2,128)S(1)}, f32[2,2,256,273]{2,0,3,1:T(2,128)}, u32[]{:S(2)}) copy-start(f32[2,2,256,273]{2,0,3,1:T(2,128)} %get-tuple-element.415) | copy-start | bytes 3354628 | tf_op jit(solution)/shard_map/while
  86.9 2.5 %copy-start.9 = (bf16[2,2,256,112]{2,3,1,0:T(8,128)(2,1)S(1)}, bf16[2,2,256,112]{2,3,1,0:T(8,128)(2,1)}, u32[]{:S(2)}) copy-start(bf16[2,2,256,112]{2,3,1,0:T(8,128)(2,1)} %get-tuple-element.393) | copy-start | bytes 688132 | tf_op jit(solution)/shard_map/while
  89.9 3.3 %copy-start.10 = (bf16[2,2,256,112]{2,3,1,0:T(8,128)(2,1)}, bf16[2,2,256,112]{2,3,1,0:T(8,128)(2,1)S(1)}, u32[]{:S(2)}) copy-start(bf16[2,2,256,112]{2,3,1,0:T(8,128)(2,1)S(1)} %fusion.139) | copy-start | bytes 688132 | tf_op jit(solution)/shard_map/while
  93.8 3.2 %copy-start.17 = (f32[2,2,256]{2,1,0:T(2,128)}, f32[2,2,256]{2,1,0:T(2,128)S(1)}, u32[]{:S(2)}) copy-start(f32[2,2,256]{2,1,0:T(2,128)S(1)} %get-tuple-element.189) | copy-start | bytes 12292
  143.3 46.7 %all-to-all-start.1 = ((bf16[8,512,224]{1,2,0:T(8,128)(2,1)}), bf16[8,512,224]{1,2,0:T(8,128)(2,1)}, u32[]{:S(2)}, u32[]{:S(2)}) async-start(bf16[8,512,224]{1,2,0:T(8,128)(2,1)} %stack.2), calls=%async_computation.2 | async-start | bytes 3670016 | tf_op jit(solution)/shard_map/all_to_all | solution.py:225
  (4 other events, 6.5 us)
Sparse Core Ops, SparseCore 0:
  10.6 54.6 all-gather.1
  99.2 41.6 reduce-scatter.1
